TPU v7x, 256 devices: a whole 4x4x8 slice. The times are simulated.
256 devices in a mesh: sa: 4 (over y), row: 4 (over x), col: 16 (over z, core).
Axes of the slice: x: 4, y: 4, z: 8, core: 2. Of those that a mesh axis runs over, the one named last changes fastest.
Arguments:
- states: float32 [2560, 1024], P(None, 'sa')
- pool: float32 [32768, 1024], P(('row', 'col'), 'sa')
- pick: int32 [16384], P(('row', 'col')), may hold values from 0 to 32767, as said below
- tile_table: int32 [8256, 2], P(('row', 'col')), may hold values from 0 to 127, as said below
Outputs:
- normal_tiles: float32 [8256, 128, 128], P(('row', 'col'), 'sa')
Inputs may be any that keep to these rules, and one draw needn't show every extreme that they name: pick[m] lies in pool rows 2 * 256 * (m // 256) to 2 * 256 * (m // 256 + 1) - 1, and the picks of one such group of 256 centres are distinct. `tile_table`: each row (i, j) has i <= j; every such pair of blocks appears in exactly one row; a row stored on the device at index r of row and c of col names one block whose centres lie on a device at row index r and another whose centres lie on a device at col index c.
All inputs are finite; a program needn't handle non-finite values.
Results may differ from a plain program's by a relative error of at most 0.00033.
Values may be sent and summed in bfloat16 or wider, within the bound.
A program may use at most 128 MiB of HBM per device.

v0:
```python
import math
import jax
import jax.numpy as jnp
from jax import lax
from jax.sharding import PartitionSpec as P

F = 1024
M = 16384
MB = 128


def squared_gap(sample_part, centre_part):
    inner_part = jnp.dot(
        sample_part,
        centre_part.T,
        precision=lax.Precision.HIGHEST,
        preferred_element_type=jnp.float32,
    )
    sample_norms = jnp.sum(sample_part * sample_part, axis=1)[:, None]
    centre_norms = jnp.sum(centre_part * centre_part, axis=1)[None, :]
    return sample_norms + centre_norms - 2.0 * inner_part


def shards(states, pool, pick, tile_table):
    sample_count = states.shape[0]
    owner_index = lax.axis_index(("row", "col"))
    centres = jnp.take(pool, pick - owner_index * pool.shape[0], axis=0)
    wide_samples = lax.all_to_all(states, "sa", split_axis=0, concat_axis=1, tiled=True)
    wide_centres = lax.all_gather(centres, "sa", axis=1, tiled=True)
    distance = squared_gap(wide_samples, wide_centres)
    kernel = jnp.exp((2.0 * F - distance) / (4.0 * math.sqrt(F))).astype(jnp.bfloat16)
    kernel_panel = lax.all_gather(kernel, ("row", "col"), axis=1, tiled=True)
    panel_blocks = kernel_panel.reshape(kernel_panel.shape[0], M // MB, MB)
    tile_count = tile_table.shape[0]
    tile_groups = tile_table.reshape(3, tile_count // 3, 2)

    def products(tile_pairs):
        left_blocks = jnp.take(panel_blocks, tile_pairs[:, 0], axis=1)
        right_blocks = jnp.take(panel_blocks, tile_pairs[:, 1], axis=1)
        summed = jnp.einsum(
            "sga,sgb->gab", left_blocks, right_blocks, preferred_element_type=jnp.float32
        )
        return summed / sample_count

    partial_tiles = lax.map(products, tile_groups).reshape(tile_count, MB, MB)
    return lax.psum_scatter(partial_tiles, "sa", scatter_dimension=1, tiled=True)


def solution(mesh):
    placed = (P(None, "sa"), P(("row", "col"), "sa"), P(("row", "col")), P(("row", "col"), None))
    return jax.shard_map(
        shards, mesh=mesh, in_specs=placed, out_specs=P(("row", "col"), "sa", None), check_vma=False
    )
```

profile of v0, /device:TPU:1, one launch (start us, length us, event | category | flops | bytes accessed | tf_op | source)
XLA Modules:
  0.0 391.3 jit_solution(11058333592931336079)
XLA Ops:
  6.5 0.0 copy-start
  6.5 5.1 %all-to-all-start = ((f32[4,640,256]{2,1,0:T(8,128)}), f32[4,640,256]{2,1,0:T(8,128)S(1)}, u32[]{:S(2)}, u32[]{:S(2)}) async-start(f32[4,640,256]{2,1,0:T(8,128)} %bitcast.55), calls=%async_computation | async-start | bytes 5242880 | tf_op jit(solution)/shard_map/all_to_all | solution.py:28
  11.7 0.0 all-gather.3.cloned.1.call-start
  11.7 0.7 compare_and_fusion.2
  12.4 0.0 copy-done
  12.4 1.0 gather_fusion.2
  13.4 0.0 copy-start.2
  13.4 0.8 broadcast_select_fusion
  14.2 0.0 all-gather.3.cloned.1.call-update
  14.2 0.0 all-gather.5.cloned.1.call-start
  14.3 36.9 %all-gather.3.cloned.1.call-done = f32[256,1024]{1,0:T(8,128)} async-done(((f32[256,256]{1,0:T(8,128)}), f32[256,1024]{1,0:T(8,128)}) %all-gather.3.cloned.1.call-update) | async-done | bytes 1048592 | tf_op jit(solution)/shard_map/all_gather | solution.py:29
  51.2 1.4 multiply_reduce_fusion.1
  52.5 0.0 all-to-all-done
  52.5 2.1 copy.12
  54.7 0.2 multiply_reduce_fusion
  54.9 5.6 %fusion.18 = bf16[640,256]{0,1:T(8,128)(2,1)} fusion(f32[256,1024]{1,0:T(8,128)} %all-gather.3.cloned.1.call-done, f32[640,1024]{0,1:T(8,128)} %bitcast.53, f32[256]{0:T(256)S(1)} %multiply_reduce_fusion.1, f32[640]{0:T(1024)S(1)} %multiply_reduce_fusion), kind=kOutput, calls=%fused_computation.27 | convolution fusion | flops 2014248960 | bytes 4001280 | tf_op jit(solution)/shard_map/dot_general | solution.py:13
  60.6 0.0 all-gather.5.cloned.1.call-update
  60.6 0.0 reduce-scatter.2.cloned.1.call-start
  60.6 0.0 copy-done.2
  60.6 0.1 reshape.24
  60.7 112.9 %all-gather.5.cloned.1.call-done = bf16[640,16384]{0,1:T(8,128)(2,1)} async-done(((bf16[640,256]{0,1:T(8,128)(2,1)}), bf16[640,16384]{0,1:T(8,128)(2,1)}) %all-gather.5.cloned.1.call-update) | async-done | bytes 20971536 | tf_op jit(solution)/shard_map/all_gather | solution.py:32
  173.6 28.2 %copy.14 = bf16[640,128,128]{2,0,1:T(8,128)(2,1)} copy(bf16[640,128,128]{0,2,1:T(8,128)(2,1)} %bitcast.52) | data formatting | bytes 41943040 | tf_op jit(solution)/shard_map/while | solution.py:45
  201.8 102.5 %while.10 = (s32[]{:T(128)}, f32[3,43,128,128]{3,2,1,0:T(8,128)}, s32[3,43,2]{1,0,2:T(4,128)S(1)}, bf16[640,128,128]{2,0,1:T(8,128)(2,1)}, s32[]{:T(128)}) while((s32[]{:T(128)}, f32[3,43,128,128]{3,2,1,0:T(8,128)}, s32[3,43,2]{1,0,2:T(4,128)S(1)}, bf16[640,128,128]{2,0,1:T(8,128)(2,1)}, s32[]{:T(128)}) %tuple.32), condition=%wide.region_3.5_spmd, body=%wide.region_2.4_spmd.sunk | while | flops 909527552 | bytes 45099772 | solution.py:45
  201.8 12.5 %gather_fusion = bf16[43,640,128]{2,1,0:T(8,128)(2,1)} fusion(bf16[640,128,128]{2,0,1:T(8,128)(2,1)} %get-tuple-element.109, s32[1024]{0:T(1024)S(1)} %get-tuple-element.92), kind=kCustom, calls=%fused_computation.1.clone.clone.1 | custom fusion | bytes 14090412 | tf_op jit(solution)/shard_map/while/body/eval_jaxpr/jit(_take)/gather | solution.py:39
  214.3 12.4 %gather_fusion.1 = bf16[43,640,128]{2,1,0:T(8,128)(2,1)} fusion(bf16[640,128,128]{2,0,1:T(8,128)(2,1)} %get-tuple-element.109, s32[1024]{0:T(1024)S(1)} %get-tuple-element.94), kind=kCustom, calls=%fused_computation.clone.clone.1 | custom fusion | bytes 14090412 | tf_op jit(solution)/shard_map/while/body/eval_jaxpr/jit(_take)/gather | solution.py:38
  226.7 9.3 %bitcast_dynamic-update-slice_fusion.2 = f32[3,43,128,128]{3,2,1,0:T(8,128)} fusion(f32[3,43,128,128]{3,2,1,0:T(8,128)} %get-tuple-element.102, s32[]{:T(128)} %get-tuple-element.101, bf16[43,640,128]{2,1,0:T(8,128)(2,1)} %gather_fusion, pred[43]{0:T(512)(128)(4,1)S(1)} %get-tuple-element.93, bf16[43,640,128]{2,1,0:T(8,128)(2,1)} %gather_fusion.1, ...), kind=kOutput, calls=%fused_computation.11.clone.1 | convolution fusion | flops 909524992 | bytes 16908886 | tf_op jit(solution)/shard_map/while/body/eval_jaxpr/sga,sgb->gab/dot_general | solution.py:40
  236.0 12.4 %gather_fusion = bf16[43,640,128]{2,1,0:T(8,128)(2,1)} fusion(bf16[640,128,128]{2,0,1:T(8,128)(2,1)} %get-tuple-element.109, s32[1024]{0:T(1024)S(1)} %get-tuple-element.92), kind=kCustom, calls=%fused_computation.1.clone.clone.1 | custom fusion | bytes 14090412 | tf_op jit(solution)/shard_map/while/body/eval_jaxpr/jit(_take)/gather | solution.py:39
  248.4 12.4 %gather_fusion.1 = bf16[43,640,128]{2,1,0:T(8,128)(2,1)} fusion(bf16[640,128,128]{2,0,1:T(8,128)(2,1)} %get-tuple-element.109, s32[1024]{0:T(1024)S(1)} %get-tuple-element.94), kind=kCustom, calls=%fused_computation.clone.clone.1 | custom fusion | bytes 14090412 | tf_op jit(solution)/shard_map/while/body/eval_jaxpr/jit(_take)/gather | solution.py:38
  260.8 9.4 %bitcast_dynamic-update-slice_fusion.2 = f32[3,43,128,128]{3,2,1,0:T(8,128)} fusion(f32[3,43,128,128]{3,2,1,0:T(8,128)} %get-tuple-element.102, s32[]{:T(128)} %get-tuple-element.101, bf16[43,640,128]{2,1,0:T(8,128)(2,1)} %gather_fusion, pred[43]{0:T(512)(128)(4,1)S(1)} %get-tuple-element.93, bf16[43,640,128]{2,1,0:T(8,128)(2,1)} %gather_fusion.1, ...), kind=kOutput, calls=%fused_computation.11.clone.1 | convolution fusion | flops 909524992 | bytes 16908886 | tf_op jit(solution)/shard_map/while/body/eval_jaxpr/sga,sgb->gab/dot_general | solution.py:40
  270.3 12.5 %gather_fusion = bf16[43,640,128]{2,1,0:T(8,128)(2,1)} fusion(bf16[640,128,128]{2,0,1:T(8,128)(2,1)} %get-tuple-element.109, s32[1024]{0:T(1024)S(1)} %get-tuple-element.92), kind=kCustom, calls=%fused_computation.1.clone.clone.1 | custom fusion | bytes 14090412 | tf_op jit(solution)/shard_map/while/body/eval_jaxpr/jit(_take)/gather | solution.py:39
  282.7 12.4 %gather_fusion.1 = bf16[43,640,128]{2,1,0:T(8,128)(2,1)} fusion(bf16[640,128,128]{2,0,1:T(8,128)(2,1)} %get-tuple-element.109, s32[1024]{0:T(1024)S(1)} %get-tuple-element.94), kind=kCustom, calls=%fused_computation.clone.clone.1 | custom fusion | bytes 14090412 | tf_op jit(solution)/shard_map/while/body/eval_jaxpr/jit(_take)/gather | solution.py:38
  295.1 9.3 %bitcast_dynamic-update-slice_fusion.2 = f32[3,43,128,128]{3,2,1,0:T(8,128)} fusion(f32[3,43,128,128]{3,2,1,0:T(8,128)} %get-tuple-element.102, s32[]{:T(128)} %get-tuple-element.101, bf16[43,640,128]{2,1,0:T(8,128)(2,1)} %gather_fusion, pred[43]{0:T(512)(128)(4,1)S(1)} %get-tuple-element.93, bf16[43,640,128]{2,1,0:T(8,128)(2,1)} %gather_fusion.1, ...), kind=kOutput, calls=%fused_computation.11.clone.1 | convolution fusion | flops 909524992 | bytes 16908886 | tf_op jit(solution)/shard_map/while/body/eval_jaxpr/sga,sgb->gab/dot_general | solution.py:40
  304.3 0.0 copy-start.1
  304.3 0.0 reduce-scatter.2.cloned.1.call-update
  304.4 80.4 %reduce-scatter.2.cloned.1.call-done = f32[129,32,128]{2,1,0:T(8,128)} async-done(((f32[129,128,128]{2,1,0:T(8,128)}), f32[129,32,128]{2,1,0:T(8,128)}) %reduce-scatter.2.cloned.1.call-update) | async-done | bytes 2113552 | tf_op jit(solution)/shard_map/reduce_scatter | solution.py:46
  384.8 0.0 copy-done.1
  (11 shorter events, 0.1 us)
Async XLA Ops:
  6.5 5.8 %copy-start = (f32[512,256]{1,0:T(8,128)S(1)}, f32[512,256]{1,0:T(8,128)}, u32[]{:S(2)}) copy-start(f32[512,256]{1,0:T(8,128)} %param.9) | copy-start | bytes 1572868
  6.5 46.0 %all-to-all-start = ((f32[4,640,256]{2,1,0:T(8,128)}), f32[4,640,256]{2,1,0:T(8,128)S(1)}, u32[]{:S(2)}, u32[]{:S(2)}) async-start(f32[4,640,256]{2,1,0:T(8,128)} %bitcast.55), calls=%async_computation | async-start | bytes 5242880 | tf_op jit(solution)/shard_map/all_to_all | solution.py:28
  11.7 39.5 %all-gather.3.cloned.1.call-start = ((), (), s32[]{:S(2)}) async-start(), calls=%async_computation.2 | async-start | bytes 1310720 | tf_op jit(solution)/shard_map/all_gather | solution.py:29
  13.4 47.3 %copy-start.2 = (s32[129,2]{0,1:T(2,128)S(1)}, s32[129,2]{0,1:T(2,128)}, u32[]{:S(2)}) copy-start(s32[129,2]{0,1:T(2,128)} %param.11) | copy-start | bytes 3100
  14.2 159.4 %all-gather.5.cloned.1.call-start = ((), (), s32[]{:S(2)}) async-start(), calls=%async_computation.3 | async-start | bytes 21299200 | tf_op jit(solution)/shard_map/all_gather | solution.py:32
  60.6 324.2 %reduce-scatter.2.cloned.1.call-start = ((), (), s32[]{:S(2)}) async-start(), calls=%async_computation.4 | async-start | bytes 10567680 | tf_op jit(solution)/shard_map/reduce_scatter | solution.py:46
  304.3 80.4 %copy-start.1 = (f32[512,256]{1,0:T(8,128)S(1)}, f32[512,256]{1,0:T(8,128)}, u32[]{:S(2)}) copy-start(f32[512,256]{1,0:T(8,128)} %param.9) | copy-start | bytes 1572868
Sparse Core Ops, SparseCore 0:
  14.3 36.7 all-gather.2
  60.7 112.8 all-gather.4
  304.5 80.2 reduce-scatter.1
where the time goes:
time: 392 us; the launch traced here: 391 us
  waiting for transfers between devices  230 us (59%)
  local copies, waits for them, and re-layouts  106 us (27%)
  matrix products  33.6 us (9%)
  between operations  13.2 us (3%)
  starting transfers between devices  5.23 us (1%)
    all_gather x1, waiting for transfers between devices, shards(): kernel_panel = lax.all_gather(kernel, ('row', 'col'), axis=1, tiled=True)  113 us
    reduce_scatter x1, waiting for transfers between devices, shards(): lax.psum_scatter(partial_tiles, 'sa', scatter_dimension=1, tiled=True)  80.4 us
    gather x3, local copies, waits for them, and re-layouts, products(): right_blocks = jnp.take(panel_blocks, tile_pairs[:, 1], axis=1)  37.3 us
    gather x3, local copies, waits for them, and re-layouts, products(): left_blocks = jnp.take(panel_blocks, tile_pairs[:, 0], axis=1)  37.1 us
    all_gather x1, waiting for transfers between devices, shards(): wide_centres = lax.all_gather(centres, 'sa', axis=1, tiled=True)  36.9 us
    while x1, local copies, waits for them, and re-layouts, shards(): partial_tiles = lax.map(products, tile_groups).reshape(tile_count, MB, MB)  28.2 us
    dot_general x3, matrix products, products(): jnp.einsum('sga,sgb->gab', left_blocks, right_blocks, preferred_element_t...  28 us
  transfers between devices with their start and end apart: 4, of which 3 were waited for; matrix products, arithmetic and copies ran while one was open for 1% of the time, Pallas kernels for 0%

commit v1 on v0

--- a/solution.py
+++ b/solution.py
@@ -29,7 +29,10 @@
     wide_centres = lax.all_gather(centres, "sa", axis=1, tiled=True)
     distance = squared_gap(wide_samples, wide_centres)
     kernel = jnp.exp((2.0 * F - distance) / (4.0 * math.sqrt(F))).astype(jnp.bfloat16)
-    kernel_panel = lax.all_gather(kernel, ("row", "col"), axis=1, tiled=True)
+    kernel_panel = jnp.concatenate(
+        lax.all_to_all(jnp.stack([kernel] * lax.axis_size(("row", "col"))), ("row", "col"), 0, 0),
+        axis=1,
+    )
     panel_blocks = kernel_panel.reshape(kernel_panel.shape[0], M // MB, MB)
     tile_count = tile_table.shape[0]
     tile_groups = tile_table.reshape(3, tile_count // 3, 2)

time: 392 us -> 754 us (1.92)
  waiting for transfers between devices: 230 us -> 573 us
  starting transfers between devices: 5.23 us -> 17.4 us
    all_to_all x0 -> x1, waiting for transfers between devices: none -> 456 us  [shards(): lax.all_to_all(jnp.stack([kernel] * lax.axis_size(('row', 'col'))), ('row...]
    all_gather x1 -> x0, waiting for transfers between devices: 113 us -> none  [shards(): kernel_panel = lax.all_gather(kernel, ('row', 'col'), axis=1, tiled=True)]
    all_to_all x0 -> x1, starting transfers between devices: none -> 12.2 us  [shards(): lax.all_to_all(jnp.stack([kernel] * lax.axis_size(('row', 'col'))), ('row...]
    another operation x0 -> x1, local copies, waits for them, and re-layouts: none -> 7.94 us  [shards(): jnp.stack([kernel] * lax.axis_size(('row', 'col')))]
where the time goes in v1:
time: 754 us; the launch traced here: 753 us
  waiting for transfers between devices  573 us (76%)
  local copies, waits for them, and re-layouts  113 us (15%)
  matrix products  32.9 us (4%)
  starting transfers between devices  17.4 us (2%)
  between operations  13.5 us (2%)
    all_to_all x1, waiting for transfers between devices, shards(): lax.all_to_all(jnp.stack([kernel] * lax.axis_size(('row', 'col'))), ('row...  456 us
    reduce_scatter x1, waiting for transfers between devices, shards(): lax.psum_scatter(partial_tiles, 'sa', scatter_dimension=1, tiled=True)  80.5 us
    gather x3, local copies, waits for them, and re-layouts, products(): right_blocks = jnp.take(panel_blocks, tile_pairs[:, 1], axis=1)  37.4 us
    gather x3, local copies, waits for them, and re-layouts, products(): left_blocks = jnp.take(panel_blocks, tile_pairs[:, 0], axis=1)  37.1 us
    all_gather x1, waiting for transfers between devices, shards(): wide_centres = lax.all_gather(centres, 'sa', axis=1, tiled=True)  37 us
    dot_general x3, matrix products, products(): jnp.einsum('sga,sgb->gab', left_blocks, right_blocks, preferred_element_t...  28 us
    while x1, local copies, waits for them, and re-layouts, shards(): partial_tiles = lax.map(products, tile_groups).reshape(tile_count, MB, MB)  27 us
  transfers between devices with their start and end apart: 4, of which 3 were waited for; matrix products, arithmetic and copies ran while one was open for 1% of the time, Pallas kernels for 0%

profile of v1, /device:TPU:1, one launch (start us, length us, event | category | flops | bytes accessed | tf_op | source)
XLA Modules:
  0.0 752.7 jit_solution(17656121695447394426)
XLA Ops:
  6.5 0.0 copy-start
  6.5 5.1 all-to-all-start
  11.7 0.0 all-gather.2.cloned.1.call-start
  11.7 0.7 compare_and_fusion.2
  12.4 0.0 copy-done
  12.4 1.0 gather_fusion.2
  13.4 0.8 broadcast_select_fusion
  14.2 0.0 all-gather.2.cloned.1.call-update
  14.2 37.0 %all-gather.2.cloned.1.call-done = f32[256,1024]{1,0:T(8,128)} async-done(((f32[256,256]{1,0:T(8,128)}), f32[256,1024]{1,0:T(8,128)}) %all-gather.2.cloned.1.call-update) | async-done | bytes 1048592 | tf_op jit(solution)/shard_map/all_gather | solution.py:29
  51.2 1.4 multiply_reduce_fusion.1
  52.5 0.0 all-to-all-done
  52.5 2.1 copy.12
  54.7 0.2 multiply_reduce_fusion
  54.9 4.9 fusion.18
  59.8 7.9 %stack.2 = bf16[64,640,256]{1,2,0:T(8,128)(2,1)} broadcast(bf16[640,256]{0,1:T(8,128)(2,1)S(1)} %fusion.18), dimensions={1,2} | broadcast | bytes 21299200 | tf_op jit(solution)/shard_map/stack | solution.py:33
  67.8 0.0 copy-start.2
  67.8 12.2 %all-to-all-start.1 = ((bf16[64,640,256]{1,2,0:T(8,128)(2,1)}), bf16[64,640,256]{1,2,0:T(8,128)(2,1)}, u32[]{:S(2)}, u32[]{:S(2)}) async-start(bf16[64,640,256]{1,2,0:T(8,128)(2,1)} %stack.2), calls=%async_computation.1 | async-start | bytes 41943040 | tf_op jit(solution)/shard_map/all_to_all | solution.py:33
  80.0 0.0 reduce-scatter.2.cloned.1.call-start
  80.1 0.0 copy-done.2
  80.1 0.1 reshape.26
  80.2 455.6 %all-to-all-done.1 = bf16[64,640,256]{1,2,0:T(8,128)(2,1)} async-done(((bf16[64,640,256]{1,2,0:T(8,128)(2,1)}), bf16[64,640,256]{1,2,0:T(8,128)(2,1)}, u32[]{:S(2)}, u32[]{:S(2)}) %all-to-all-start.1) | async-done | bytes 20971552 | tf_op jit(solution)/shard_map/all_to_all | solution.py:33
  535.8 27.0 %copy.14 = bf16[640,128,128]{2,0,1:T(8,128)(2,1)} copy(bf16[640,128,128]{0,2,1:T(8,128)(2,1)} %bitcast.11) | data formatting | bytes 41943040 | tf_op jit(solution)/shard_map/while | solution.py:48
  562.8 102.5 %while.10 = (s32[]{:T(128)}, f32[3,43,128,128]{3,2,1,0:T(8,128)}, s32[3,43,2]{1,0,2:T(4,128)S(1)}, bf16[640,128,128]{2,0,1:T(8,128)(2,1)}, s32[]{:T(128)}) while((s32[]{:T(128)}, f32[3,43,128,128]{3,2,1,0:T(8,128)}, s32[3,43,2]{1,0,2:T(4,128)S(1)}, bf16[640,128,128]{2,0,1:T(8,128)(2,1)}, s32[]{:T(128)}) %tuple.31), condition=%wide.region_3.5_spmd, body=%wide.region_2.4_spmd.sunk | while | flops 909527552 | bytes 45099772 | solution.py:48
  562.8 12.5 %gather_fusion = bf16[43,640,128]{2,1,0:T(8,128)(2,1)} fusion(bf16[640,128,128]{2,0,1:T(8,128)(2,1)} %get-tuple-element.105, s32[1024]{0:T(1024)S(1)} %get-tuple-element.88), kind=kCustom, calls=%fused_computation.1.clone.clone.1 | custom fusion | bytes 14090412 | tf_op jit(solution)/shard_map/while/body/eval_jaxpr/jit(_take)/gather | solution.py:42
  575.3 12.4 %gather_fusion.1 = bf16[43,640,128]{2,1,0:T(8,128)(2,1)} fusion(bf16[640,128,128]{2,0,1:T(8,128)(2,1)} %get-tuple-element.105, s32[1024]{0:T(1024)S(1)} %get-tuple-element.90), kind=kCustom, calls=%fused_computation.clone.clone.1 | custom fusion | bytes 14090412 | tf_op jit(solution)/shard_map/while/body/eval_jaxpr/jit(_take)/gather | solution.py:41
  587.7 9.3 %bitcast_dynamic-update-slice_fusion.2 = f32[3,43,128,128]{3,2,1,0:T(8,128)} fusion(f32[3,43,128,128]{3,2,1,0:T(8,128)} %get-tuple-element.98, s32[]{:T(128)} %get-tuple-element.97, bf16[43,640,128]{2,1,0:T(8,128)(2,1)} %gather_fusion, pred[43]{0:T(512)(128)(4,1)S(1)} %get-tuple-element.89, bf16[43,640,128]{2,1,0:T(8,128)(2,1)} %gather_fusion.1, ...), kind=kOutput, calls=%fused_computation.11.clone.1 | convolution fusion | flops 909524992 | bytes 16908886 | tf_op jit(solution)/shard_map/while/body/eval_jaxpr/sga,sgb->gab/dot_general | solution.py:43
  597.0 12.4 %gather_fusion = bf16[43,640,128]{2,1,0:T(8,128)(2,1)} fusion(bf16[640,128,128]{2,0,1:T(8,128)(2,1)} %get-tuple-element.105, s32[1024]{0:T(1024)S(1)} %get-tuple-element.88), kind=kCustom, calls=%fused_computation.1.clone.clone.1 | custom fusion | bytes 14090412 | tf_op jit(solution)/shard_map/while/body/eval_jaxpr/jit(_take)/gather | solution.py:42
  609.4 12.4 %gather_fusion.1 = bf16[43,640,128]{2,1,0:T(8,128)(2,1)} fusion(bf16[640,128,128]{2,0,1:T(8,128)(2,1)} %get-tuple-element.105, s32[1024]{0:T(1024)S(1)} %get-tuple-element.90), kind=kCustom, calls=%fused_computation.clone.clone.1 | custom fusion | bytes 14090412 | tf_op jit(solution)/shard_map/while/body/eval_jaxpr/jit(_take)/gather | solution.py:41
  621.8 9.4 %bitcast_dynamic-update-slice_fusion.2 = f32[3,43,128,128]{3,2,1,0:T(8,128)} fusion(f32[3,43,128,128]{3,2,1,0:T(8,128)} %get-tuple-element.98, s32[]{:T(128)} %get-tuple-element.97, bf16[43,640,128]{2,1,0:T(8,128)(2,1)} %gather_fusion, pred[43]{0:T(512)(128)(4,1)S(1)} %get-tuple-element.89, bf16[43,640,128]{2,1,0:T(8,128)(2,1)} %gather_fusion.1, ...), kind=kOutput, calls=%fused_computation.11.clone.1 | convolution fusion | flops 909524992 | bytes 16908886 | tf_op jit(solution)/shard_map/while/body/eval_jaxpr/sga,sgb->gab/dot_general | solution.py:43
  631.3 12.5 %gather_fusion = bf16[43,640,128]{2,1,0:T(8,128)(2,1)} fusion(bf16[640,128,128]{2,0,1:T(8,128)(2,1)} %get-tuple-element.105, s32[1024]{0:T(1024)S(1)} %get-tuple-element.88), kind=kCustom, calls=%fused_computation.1.clone.clone.1 | custom fusion | bytes 14090412 | tf_op jit(solution)/shard_map/while/body/eval_jaxpr/jit(_take)/gather | solution.py:42
  643.7 12.4 %gather_fusion.1 = bf16[43,640,128]{2,1,0:T(8,128)(2,1)} fusion(bf16[640,128,128]{2,0,1:T(8,128)(2,1)} %get-tuple-element.105, s32[1024]{0:T(1024)S(1)} %get-tuple-element.90), kind=kCustom, calls=%fused_computation.clone.clone.1 | custom fusion | bytes 14090412 | tf_op jit(solution)/shard_map/while/body/eval_jaxpr/jit(_take)/gather | solution.py:41
  656.1 9.3 %bitcast_dynamic-update-slice_fusion.2 = f32[3,43,128,128]{3,2,1,0:T(8,128)} fusion(f32[3,43,128,128]{3,2,1,0:T(8,128)} %get-tuple-element.98, s32[]{:T(128)} %get-tuple-element.97, bf16[43,640,128]{2,1,0:T(8,128)(2,1)} %gather_fusion, pred[43]{0:T(512)(128)(4,1)S(1)} %get-tuple-element.89, bf16[43,640,128]{2,1,0:T(8,128)(2,1)} %gather_fusion.1, ...), kind=kOutput, calls=%fused_computation.11.clone.1 | convolution fusion | flops 909524992 | bytes 16908886 | tf_op jit(solution)/shard_map/while/body/eval_jaxpr/sga,sgb->gab/dot_general | solution.py:43
  665.3 0.0 copy-start.1
  665.3 0.0 reduce-scatter.2.cloned.1.call-update
  665.4 80.5 %reduce-scatter.2.cloned.1.call-done = f32[129,32,128]{2,1,0:T(8,128)} async-done(((f32[129,128,128]{2,1,0:T(8,128)}), f32[129,32,128]{2,1,0:T(8,128)}) %reduce-scatter.2.cloned.1.call-update) | async-done | bytes 2113552 | tf_op jit(solution)/shard_map/reduce_scatter | solution.py:49
  745.9 0.0 copy-done.1
  (11 shorter events, 0.1 us)
Async XLA Ops:
  6.5 5.8 copy-start
  6.5 46.0 %all-to-all-start = ((f32[4,640,256]{2,1,0:T(8,128)}), f32[4,640,256]{2,1,0:T(8,128)S(1)}, u32[]{:S(2)}, u32[]{:S(2)}) async-start(f32[4,640,256]{2,1,0:T(8,128)} %bitcast.56), calls=%async_computation | async-start | bytes 5242880 | tf_op jit(solution)/shard_map/all_to_all | solution.py:28
  11.7 39.5 %all-gather.2.cloned.1.call-start = ((), (), s32[]{:S(2)}) async-start(), calls=%async_computation.3 | async-start | bytes 1310720 | tf_op jit(solution)/shard_map/all_gather | solution.py:29
  67.8 12.3 %copy-start.2 = (s32[129,2]{0,1:T(2,128)S(1)}, s32[129,2]{0,1:T(2,128)}, u32[]{:S(2)}) copy-start(s32[129,2]{0,1:T(2,128)} %param.11) | copy-start | bytes 3100
  67.8 468.0 %all-to-all-start.1 = ((bf16[64,640,256]{1,2,0:T(8,128)(2,1)}), bf16[64,640,256]{1,2,0:T(8,128)(2,1)}, u32[]{:S(2)}, u32[]{:S(2)}) async-start(bf16[64,640,256]{1,2,0:T(8,128)(2,1)} %stack.2), calls=%async_computation.1 | async-start | bytes 41943040 | tf_op jit(solution)/shard_map/all_to_all | solution.py:33
  80.0 665.8 %reduce-scatter.2.cloned.1.call-start = ((), (), s32[]{:S(2)}) async-start(), calls=%async_computation.4 | async-start | bytes 10567680 | tf_op jit(solution)/shard_map/reduce_scatter | solution.py:49
  665.3 80.5 %copy-start.1 = (f32[512,256]{1,0:T(8,128)S(1)}, f32[512,256]{1,0:T(8,128)}, u32[]{:S(2)}) copy-start(f32[512,256]{1,0:T(8,128)} %param.9) | copy-start | bytes 1572868
Sparse Core Ops, SparseCore 0:
  14.3 36.8 all-gather.1
  665.5 80.3 reduce-scatter.1
